TPU v7x, 32 devices: a whole 2x2x4 slice. The times are simulated.
32 devices in a mesh: phase: 4 (over x, core), seq: 4 (over z), mp: 2 (over y).
Axes of the slice: x: 2, y: 2, z: 4, core: 2. Of those that a mesh axis runs over, the one named last changes fastest.
Arguments:
- queries: bfloat16 [4, 2048, 4096], P('phase', 'seq', 'mp'), may hold values from -360 to 360
- key_weight: bfloat16 [4, 1024, 4096], P('phase', None, 'mp'), may hold values from -0.1875 to 0.1875
- value_weight: bfloat16 [4, 1024, 4096], P('phase', None, 'mp'), may hold values from -0.1875 to 0.1875
- enc_gain: float32 [1024], replicated, may hold values from 0.25 to 2
- neighbour_states: bfloat16 [80, 64, 1024], P('seq', ('phase', 'mp')), may hold values from -600 to 600
- slot_dest: int32 [80], P('seq'), may hold values from -1 to 63, as said below
Outputs:
- context: bfloat16 [4, 2048, 4096], P('phase', 'seq', 'mp')
Inputs may be any that keep to these rules, and one draw needn't show every extreme that they name: slot_dest names every position 0 to 63 exactly once and is -1 elsewhere. Positions 2 * 8 j to 2 * 8 (j + 1) - 1 belong to the tokens of index j of seq. The slots of one index of seq name at most 5 positions of any one index of seq, and this bound is reached; one index of seq has up to 20 filled slots, reached in every draw.
All inputs are finite; a program needn't handle non-finite values.
Results may differ from a plain program's by a relative error of at most 0.0074.
Values may be sent and summed in bfloat16 or wider, within the bound.
No kernel may reach another device: no remote copies, remote signals or barrier semaphores. Data moves between devices by JAX's collectives and lax.ppermute only.
A program may use at most 64 MiB of HBM per device.

v0:
```python
import jax
import jax.numpy as jnp
from jax import lax
from jax.sharding import PartitionSpec as P

HD = 128
SEGLEN = 64
NLEN = 64
NEIGH = 2


def shifted(shard, axis, by):
    peers = lax.axis_size(axis)
    pairs = [(i, i + by) for i in range(peers) if 0 <= i + by < peers]
    return lax.ppermute(shard, axis, pairs)


def normalize(rows, gain):
    states = rows.astype(jnp.float32)
    meansq = jnp.mean(states * states, axis=-1, keepdims=True)
    return (states * lax.rsqrt(meansq + 1e-06) * gain).astype(jnp.bfloat16)


def project(rows, weight):
    flattened = rows.reshape(-1, rows.shape[-1])
    return jnp.dot(flattened, weight, preferred_element_type=jnp.float32).astype(jnp.bfloat16)


def attend(query_win, key_win, value_win):
    windows = query_win.shape[0]
    heads = query_win.shape[2] // HD
    query_four = query_win.reshape(windows, query_win.shape[1], heads, HD)
    key_four = key_win.reshape(windows, key_win.shape[1], heads, HD)
    value_four = value_win.reshape(windows, value_win.shape[1], heads, HD)
    scores = jnp.einsum(
        "wqhd,wkhd->whqk", query_four, key_four, preferred_element_type=jnp.float32
    ) * HD ** (-0.5)
    top = jnp.max(scores, axis=-1, keepdims=True)
    exponent = jnp.exp(scores - top)
    weights = (exponent / jnp.sum(exponent, axis=-1, keepdims=True)).astype(jnp.bfloat16)
    context = jnp.einsum("whqk,wkhd->wqhd", weights, value_four, preferred_element_type=jnp.float32)
    return context.astype(jnp.bfloat16).reshape(windows, query_win.shape[1], heads * HD)


def packing(slot_dest, shards, per_shard, capacity):
    count = slot_dest.shape[0]
    is_live = slot_dest >= 0
    target = jnp.where(is_live, slot_dest // per_shard, -1)
    order = jnp.arange(count)
    earlier = (target[:, None] == target[None, :]) & (order[None, :] < order[:, None])
    slot_rank = jnp.sum(earlier.astype(jnp.int32), axis=1)
    buffer_slot = jnp.where(is_live, target * capacity + slot_rank, -1)
    matches = jnp.arange(shards * capacity)[:, None] == buffer_slot[None, :]
    selector = matches.astype(jnp.bfloat16)
    sent_dest = jnp.sum(jnp.where(matches, slot_dest[None, :] + 1, 0), axis=1) - 1
    return (selector, sent_dest.reshape(shards, capacity))


def pack(selector, rows, shards, capacity):
    flattened = rows.reshape(rows.shape[0], rows.shape[1] * rows.shape[2])
    packed = jnp.dot(selector, flattened, preferred_element_type=jnp.float32).astype(jnp.bfloat16)
    return packed.reshape(shards, capacity, rows.shape[1], rows.shape[2])


def unpack(received, received_dest, own_index, per_shard):
    flat_dest = received_dest.reshape(-1)
    local = jnp.where(flat_dest >= 0, flat_dest - own_index * per_shard, -1)
    placer = (jnp.arange(per_shard)[:, None] == local[None, :]).astype(jnp.bfloat16)
    stacked = received.reshape(flat_dest.shape[0], received.shape[2] * received.shape[3])
    placed = jnp.dot(placer, stacked, preferred_element_type=jnp.float32).astype(jnp.bfloat16)
    return placed.reshape(per_shard, received.shape[2], received.shape[3])


def edge_windows(query_rows, keys, values, prev_keys, prev_values):
    tokens_here = query_rows.shape[0]
    width = query_rows.shape[1]
    blocks = keys.shape[0]
    padded = jnp.concatenate(
        [
            jnp.zeros((1, width), jnp.bfloat16),
            query_rows,
            jnp.zeros((SEGLEN - 1, width), jnp.bfloat16),
        ],
        axis=0,
    )
    padded = padded.reshape(blocks + 1, SEGLEN, width)
    all_keys = jnp.concatenate([prev_keys[None], keys], axis=0)
    all_values = jnp.concatenate([prev_values[None], values], axis=0)
    context = attend(padded, all_keys, all_values)
    return context.reshape((blocks + 1) * SEGLEN, width)[1 : tokens_here + 1]


def on_device(queries, key_weight, value_weight, enc_gain, neighbour_states, slot_dest):
    shards = lax.axis_size("seq")
    own_index = lax.axis_index("seq")
    query_rows = queries[0]
    tokens_here = query_rows.shape[0]
    blocks = tokens_here // SEGLEN
    per_shard = NEIGH * blocks
    capacity = per_shard // shards + 1
    selector, sent_dest = packing(slot_dest, shards, per_shard, capacity)
    received, received_dest = (
        lax.all_to_all(
            pack(selector, neighbour_states, shards, capacity),
            "seq",
            split_axis=0,
            concat_axis=0,
            tiled=True,
        ),
        lax.all_to_all(sent_dest, "seq", split_axis=0, concat_axis=0, tiled=True),
    )
    arranged = unpack(received, received_dest, own_index, per_shard)
    routed = lax.all_gather(arranged, ("phase", "mp"), axis=1, tiled=True)
    neighbours = normalize(routed, enc_gain)
    key_mat = key_weight[0]
    value_mat = value_weight[0]
    width = key_mat.shape[1]
    keys = project(neighbours, key_mat).reshape(blocks, NEIGH * NLEN, width)
    values = project(neighbours, value_mat).reshape(blocks, NEIGH * NLEN, width)
    prev_keys, prev_values = shifted((keys[blocks - 1], values[blocks - 1]), "seq", 1)
    joined = edge_windows(query_rows, keys, values, prev_keys, prev_values)
    position = jnp.arange(tokens_here) + 1
    window_index = own_index * blocks + position // SEGLEN
    silent = (position % SEGLEN != 0) & (window_index == 0)
    result = jnp.where(silent[:, None], jnp.zeros_like(joined), joined)
    return result[None]


def solution(mesh):
    in_specs = (
        P("phase", "seq", "mp"),
        P("phase", None, "mp"),
        P("phase", None, "mp"),
        P(),
        P("seq", ("phase", "mp"), None),
        P("seq"),
    )
    out_specs = P("phase", "seq", "mp")
    return jax.shard_map(
        on_device, mesh=mesh, in_specs=in_specs, out_specs=out_specs, check_vma=False
    )
```

profile of v0, /device:TPU:0, one launch (start us, length us, event | category | flops | bytes accessed | tf_op | source)
XLA Modules:
  0.0 137.3 jit_solution(5685725750526515950)
XLA Ops:
  6.5 0.7 broadcast_add_fusion.1
  7.2 0.2 convert_reduce_fusion
  7.4 0.7 compare_select_fusion.4
  8.0 0.1 select_reduce_fusion
  8.2 0.7 sub.37
  8.8 6.3 %all-to-all-start = ((s32[4,1,5]{2,1,0:T(1,128)}), s32[4,1,5]{2,1,0:T(1,128)S(1)}, u32[]{:S(2)}, u32[]{:S(2)}) async-start(s32[4,1,5]{2,1,0:T(1,128)} %bitcast), calls=%async_computation | async-start | bytes 4096 | tf_op jit(solution)/shard_map/all_to_all | solution.py:110
  15.2 1.0 pad.7
  16.2 0.0 copy-start.6
  16.2 0.2 copy.32
  16.4 0.3 convolution_convert_fusion
  16.7 0.2 copy.33
  16.9 0.7 slice.17
  17.7 2.9 %all-to-all-done = s32[4,1,5]{2,1,0:T(1,128)S(1)} async-done(((s32[4,1,5]{2,1,0:T(1,128)}), s32[4,1,5]{2,1,0:T(1,128)S(1)}, u32[]{:S(2)}, u32[]{:S(2)}) %all-to-all-start) | async-done | bytes 112 | tf_op jit(solution)/shard_map/all_to_all | solution.py:110
  20.6 3.5 %all-to-all-start.1 = ((bf16[4,5,8,1024]{3,2,1,0:T(8,128)(2,1)}), bf16[4,5,8,1024]{3,2,1,0:T(8,128)(2,1)S(1)}, u32[]{:S(2)}, u32[]{:S(2)}) async-start(bf16[4,5,8,1024]{3,2,1,0:T(8,128)(2,1)} %bitcast.17), calls=%async_computation.1 | async-start | bytes 655360 | tf_op jit(solution)/shard_map/all_to_all | solution.py:103
  24.1 0.0 all-gather.2.cloned.1.call-start
  24.2 0.1 select_n.57
  24.2 9.1 %all-to-all-done.1 = bf16[4,5,8,1024]{3,2,1,0:T(8,128)(2,1)S(1)} async-done(((bf16[4,5,8,1024]{3,2,1,0:T(8,128)(2,1)}), bf16[4,5,8,1024]{3,2,1,0:T(8,128)(2,1)S(1)}, u32[]{:S(2)}, u32[]{:S(2)}) %all-to-all-start.1) | async-done | bytes 327712 | tf_op jit(solution)/shard_map/all_to_all | solution.py:103
  33.4 0.2 copy.34
  33.6 0.2 convolution_convert_fusion.1
  33.8 0.9 copy.35
  34.7 0.0 all-gather.2.cloned.1.call-update
  34.7 27.0 %all-gather.2.cloned.1.call-done = bf16[16,64,1024]{2,1,0:T(8,128)(2,1)} async-done(((bf16[16,8,1024]{2,1,0:T(8,128)(2,1)}), bf16[16,64,1024]{2,1,0:T(8,128)(2,1)}) %all-gather.2.cloned.1.call-update) | async-done | bytes 2097168 | tf_op jit(solution)/shard_map/all_gather | solution.py:113
  61.7 0.0 copy-start.7
  61.7 2.2 %fusion.9 = f32[16,64]{1,0:T(8,128)S(1)} fusion(bf16[16,64,1024]{2,1,0:T(8,128)(2,1)} %all-gather.2.cloned.1.call-done), kind=kLoop, calls=%fused_computation.15 | loop fusion | flops 3144704 | bytes 2101248 | tf_op jit(solution)/shard_map/reduce_sum | solution.py:20
  64.0 0.0 copy-done.6
  64.0 2.1 %fusion.11 = bf16[16,64,1024]{2,1,0:T(8,128)(2,1)S(1)} fusion(bf16[16,64,1024]{2,1,0:T(8,128)(2,1)} %all-gather.2.cloned.1.call-done, f32[1024]{0:T(1024)S(1)} %copy-done.6, f32[16,64]{1,0:T(8,128)S(1)} %add_rsqrt_fusion), kind=kLoop, calls=%fused_computation.17 | loop fusion | flops 4194304 | bytes 4202496 | tf_op jit(solution)/shard_map/convert_element_type | solution.py:21
  66.1 0.0 copy-done.7
  66.1 0.0 copy-start.8
  66.1 4.7 %fusion.20 = bf16[1024,2048]{1,0:T(8,128)(2,1)S(1)} fusion(bf16[1024,1024]{1,0:T(8,128)(2,1)S(1)} %bitcast.64, bf16[1,1024,2048]{2,1,0:T(8,128)(2,1)S(1)} %copy-done.7), kind=kOutput, calls=%fused_computation.25 | convolution fusion | flops 4297064448 | bytes 10485760 | tf_op jit(solution)/shard_map/dot_general | solution.py:26
  70.9 0.0 copy-start
  70.9 0.9 slice.14
  71.8 0.0 copy-start.5
  71.8 3.7 %collective-permute-start.1 = (bf16[128,2048]{1,0:T(8,128)(2,1)}, bf16[128,2048]{1,0:T(8,128)(2,1)S(1)}, u32[]{:S(2)}, u32[]{:S(2)}) collective-permute-start(bf16[128,2048]{1,0:T(8,128)(2,1)} %slice.14), channel_id=1, source_target_pairs={{0,2},{2,4},{4,6},{1,3},{3,5},{5,7},{8,10},{10,12},{12,14},{9,11},... | collective-permute-start | bytes 1572872 | tf_op jit(solution)/shard_map/ppermute | solution.py:15
  75.4 0.0 copy-done.8
  75.4 4.7 %fusion.17 = bf16[1024,2048]{1,0:T(8,128)(2,1)S(1)} fusion(bf16[1024,1024]{1,0:T(8,128)(2,1)S(1)} %bitcast.65, bf16[1,1024,2048]{2,1,0:T(8,128)(2,1)S(1)} %copy-done.8), kind=kOutput, calls=%fused_computation.24 | convolution fusion | flops 4297064448 | bytes 10485760 | tf_op jit(solution)/shard_map/dot_general | solution.py:26
  80.2 0.0 copy-done
  80.2 0.0 copy-start.2
  80.2 0.9 slice.15
  81.1 1.3 copy-done.2
  82.4 3.6 %collective-permute-start = (bf16[128,2048]{1,0:T(8,128)(2,1)}, bf16[128,2048]{1,0:T(8,128)(2,1)S(1)}, u32[]{:S(2)}, u32[]{:S(2)}) collective-permute-start(bf16[128,2048]{1,0:T(8,128)(2,1)} %slice.15), channel_id=1, source_target_pairs={{0,2},{2,4},{4,6},{1,3},{3,5},{5,7},{8,10},{10,12},{12,14},{9,11},... | collective-permute-start | bytes 1572872 | tf_op jit(solution)/shard_map/ppermute | solution.py:15
  86.0 0.1 pad.6.clone
  86.0 0.0 copy-done.5
  86.0 1.0 maximum_bitcast_fusion
  87.1 0.7 copy.31
  87.8 0.4 copy-done.3
  88.2 1.4 %copy.39 = bf16[128,8,16,128]{3,2,1,0:T(8,128)(2,1)S(1)} copy(bf16[128,8,16,128]{3,1,2,0:T(8,128)(2,1)S(1)} %bitcast.62) | data formatting | bytes 8388608
  89.6 0.0 copy-start.1
  89.7 3.2 %copy.26 = bf16[8,128,16,128]{3,1,2,0:T(8,128)(2,1)} copy(bf16[8,128,16,128]{3,2,1,0:T(8,128)(2,1)S(1)} %bitcast.56) | data formatting | bytes 8388608 | tf_op jit(solution)/shard_map/concatenate | solution.py:88
  92.8 0.0 copy-done.1
  92.8 1.4 %copy.37 = bf16[128,8,16,128]{3,2,1,0:T(8,128)(2,1)S(1)} copy(bf16[128,8,16,128]{3,1,2,0:T(8,128)(2,1)S(1)} %bitcast.61) | data formatting | bytes 8388608
  94.3 1.2 copy.28
  95.4 0.0 collective-permute-done.1
  95.4 0.1 copy.36
  95.6 0.1 copy.27
  95.7 2.8 %collective-permute-done = bf16[128,2048]{1,0:T(8,128)(2,1)S(1)} collective-permute-done((bf16[128,2048]{1,0:T(8,128)(2,1)}, bf16[128,2048]{1,0:T(8,128)(2,1)S(1)}, u32[]{:S(2)}, u32[]{:S(2)}) %collective-permute-start) | collective-permute-done | bytes 524320 | tf_op jit(solution)/shard_map/ppermute | solution.py:15
  98.5 0.1 copy.38
  98.6 0.1 copy.25
  98.8 3.3 %fusion.1 = f32[9,16,64,128]{3,2,1,0:T(8,128)S(1)} fusion(bf16[8,128,16,128]{3,1,2,0:T(8,128)(2,1)S(1)} %copy.28, bf16[1,128,16,128]{3,1,2,0:T(8,128)(2,1)S(1)} %copy.27, bf16[9,64,16,128]{3,2,1,0:T(8,128)(2,1)S(1)} %bitcast.59), kind=kOutput, calls=%fused_computation.5 | convolution fusion | flops 304349184 | bytes 11796480 | tf_op jit(solution)/shard_map/wqhd,wkhd->whqk/dot_general | solution.py:35
  102.1 2.1 %copy-done.4 = f32[9,16,64,128]{3,2,1,0:T(8,128)} copy-done((f32[9,16,64,128]{3,2,1,0:T(8,128)}, f32[9,16,64,128]{3,2,1,0:T(8,128)S(1)}, u32[]{:S(2)}) %copy-start.4) | copy-done | bytes 4718616
  104.2 2.5 %fusion.51 = f32[9,16,64]{2,1,0:T(8,128)S(1)} fusion(f32[9,16,64,128]{3,2,1,0:T(8,128)S(1)} %fusion.1), kind=kOutput, calls=%fused_computation.71 | output fusion | flops 4718719 | bytes 4755456 | tf_op jit(solution)/shard_map/sub | solution.py:39
  106.7 19.5 %convert_bitcast_fusion = bf16[9,64,16,128]{3,1,2,0:T(8,128)(2,1)S(1)} fusion(bf16[8,128,16,128]{3,1,2,0:T(8,128)(2,1)} %copy.26, bf16[1,128,16,128]{3,1,2,0:T(8,128)(2,1)S(1)} %copy.25, f32[9,16,64]{2,1,0:T(8,128)S(1)} %fusion.51, f32[9,16,64,128]{3,2,1,0:T(8,128)} %copy-done.4), kind=kOutput, calls=%fused_computation.29 | convolution fusion | flops 318514304 | bytes 11833344 | tf_op jit(solution)/shard_map/whqk,wkhd->wqhd/dot_general | solution.py:41
  126.2 1.6 %copy.30 = bf16[9,64,16,128]{3,2,1,0:T(8,128)(2,1)S(1)} copy(bf16[9,64,16,128]{3,1,2,0:T(8,128)(2,1)S(1)} %convert_bitcast_fusion) | data formatting | bytes 4718592 | tf_op jit(solution)/shard_map/convert_element_type | solution.py:42
  127.8 0.6 copy.44
  128.5 2.0 %fusion.28 = bf16[1,512,2048]{2,1,0:T(8,128)(2,1)} fusion(bf16[576,2048]{1,0:T(8,128)(2,1)S(1)} %bitcast.60, pred[512]{0:T(512)(128)(4,1)S(1)} %fusion.44), kind=kLoop, calls=%fused_computation.33 | loop fusion | flops 1048576 | bytes 4194816 | tf_op jit(solution)/shard_map/broadcast_in_dim | solution.py:126
  (9 shorter events, 0.1 us)
Async XLA Ops:
  8.8 11.8 %all-to-all-start = ((s32[4,1,5]{2,1,0:T(1,128)}), s32[4,1,5]{2,1,0:T(1,128)S(1)}, u32[]{:S(2)}, u32[]{:S(2)}) async-start(s32[4,1,5]{2,1,0:T(1,128)} %bitcast), calls=%async_computation | async-start | bytes 4096 | tf_op jit(solution)/shard_map/all_to_all | solution.py:110
  16.2 47.8 %copy-start.6 = (f32[1024]{0:T(1024)S(1)}, f32[1024]{0:T(1024)}, u32[]{:S(2)}) copy-start(f32[1024]{0:T(1024)} %param.9) | copy-start | bytes 12292
  20.6 12.7 %all-to-all-start.1 = ((bf16[4,5,8,1024]{3,2,1,0:T(8,128)(2,1)}), bf16[4,5,8,1024]{3,2,1,0:T(8,128)(2,1)S(1)}, u32[]{:S(2)}, u32[]{:S(2)}) async-start(bf16[4,5,8,1024]{3,2,1,0:T(8,128)(2,1)} %bitcast.17), calls=%async_computation.1 | async-start | bytes 655360 | tf_op jit(solution)/shard_map/all_to_all | solution.py:103
  24.1 37.6 %all-gather.2.cloned.1.call-start = ((), (), s32[]{:S(2)}) async-start(), calls=%async_computation.2 | async-start | bytes 2359296 | tf_op jit(solution)/shard_map/all_gather | solution.py:113
  61.7 4.4 %copy-start.7 = (bf16[1,1024,2048]{2,1,0:T(8,128)(2,1)S(1)}, bf16[1,1024,2048]{2,1,0:T(8,128)(2,1)}, u32[]{:S(2)}) copy-start(bf16[1,1024,2048]{2,1,0:T(8,128)(2,1)} %param.7) | copy-start | bytes 12582916
  66.1 9.3 %copy-start.8 = (bf16[1,1024,2048]{2,1,0:T(8,128)(2,1)S(1)}, bf16[1,1024,2048]{2,1,0:T(8,128)(2,1)}, u32[]{:S(2)}) copy-start(bf16[1,1024,2048]{2,1,0:T(8,128)(2,1)} %param.8) | copy-start | bytes 12582916
  70.9 9.3 %copy-start = (bf16[1024,2048]{1,0:T(8,128)(2,1)}, bf16[1024,2048]{1,0:T(8,128)(2,1)S(1)}, u32[]{:S(2)}) copy-start(bf16[1024,2048]{1,0:T(8,128)(2,1)S(1)} %fusion.20) | copy-start | bytes 12582916
  71.8 14.3 %copy-start.5 = (bf16[1,512,2048]{2,1,0:T(8,128)(2,1)S(1)}, bf16[1,512,2048]{2,1,0:T(8,128)(2,1)}, u32[]{:S(2)}) copy-start(bf16[1,512,2048]{2,1,0:T(8,128)(2,1)} %param.6) | copy-start | bytes 6291460
  71.8 23.7 %collective-permute-start.1 = (bf16[128,2048]{1,0:T(8,128)(2,1)}, bf16[128,2048]{1,0:T(8,128)(2,1)S(1)}, u32[]{:S(2)}, u32[]{:S(2)}) collective-permute-start(bf16[128,2048]{1,0:T(8,128)(2,1)} %slice.14), channel_id=1, source_target_pairs={{0,2},{2,4},{4,6},{1,3},{3,5},{5,7},{8,10},{10,12},{12,14},{9,11},... | collective-permute-start | bytes 1572872 | tf_op jit(solution)/shard_map/ppermute | solution.py:15
  80.2 2.2 %copy-start.2 = (bf16[1024,2048]{1,0:T(8,128)(2,1)}, bf16[1024,2048]{1,0:T(8,128)(2,1)S(1)}, u32[]{:S(2)}) copy-start(bf16[1024,2048]{1,0:T(8,128)(2,1)S(1)} %fusion.17) | copy-start | bytes 12582916
  82.4 16.1 %collective-permute-start = (bf16[128,2048]{1,0:T(8,128)(2,1)}, bf16[128,2048]{1,0:T(8,128)(2,1)S(1)}, u32[]{:S(2)}, u32[]{:S(2)}) collective-permute-start(bf16[128,2048]{1,0:T(8,128)(2,1)} %slice.15), channel_id=1, source_target_pairs={{0,2},{2,4},{4,6},{1,3},{3,5},{5,7},{8,10},{10,12},{12,14},{9,11},... | collective-permute-start | bytes 1572872 | tf_op jit(solution)/shard_map/ppermute | solution.py:15
  86.0 2.2 %copy-start.3 = (bf16[1024,2048]{1,0:T(8,128)(2,1)S(1)}, bf16[1024,2048]{1,0:T(8,128)(2,1)}, u32[]{:S(2)}) copy-start(bf16[1024,2048]{1,0:T(8,128)(2,1)} %copy-done.2) | copy-start | bytes 12582916
  89.6 3.2 %copy-start.1 = (bf16[1024,2048]{1,0:T(8,128)(2,1)S(1)}, bf16[1024,2048]{1,0:T(8,128)(2,1)}, u32[]{:S(2)}) copy-start(bf16[1024,2048]{1,0:T(8,128)(2,1)} %copy-done) | copy-start | bytes 12582916
  102.1 2.1 %copy-start.4 = (f32[9,16,64,128]{3,2,1,0:T(8,128)}, f32[9,16,64,128]{3,2,1,0:T(8,128)S(1)}, u32[]{:S(2)}) copy-start(f32[9,16,64,128]{3,2,1,0:T(8,128)S(1)} %fusion.1) | copy-start | bytes 14155780
Sparse Core Ops, SparseCore 0:
  34.8 26.8 all-gather.1
where the time goes:
time: 138 us; the launch traced here: 137 us
  waiting for transfers between devices  41.9 us (30%)
  matrix products  32.7 us (24%)
  local copies, waits for them, and re-layouts  20.4 us (15%)
  starting transfers between devices  17.1 us (12%)
  between operations  13.7 us (10%)
  other arithmetic  11.6 us (8%)
    all_gather x1, waiting for transfers between devices, on_device(): routed = lax.all_gather(arranged, ('phase', 'mp'), axis=1, tiled=True)  27 us
    dot_general x1, matrix products, attend(): jnp.einsum('whqk,wkhd->wqhd', weights, value_four, preferred_element_type...  19.5 us
    unnamed x31, local copies, waits for them, and re-layouts  11.5 us
    dot_general x2, matrix products, project(): jnp.dot(flattened, weight, preferred_element_type=jnp.float32)  9.46 us
    all_to_all x1, waiting for transfers between devices, on_device(): lax.all_to_all(pack(selector, neighbour_states, shards, capacity), 'seq',...  9.08 us
    ppermute x2, starting transfers between devices, shifted(): return lax.ppermute(shard, axis, pairs)  7.23 us
    all_to_all x1, starting transfers between devices, on_device(): lax.all_to_all(sent_dest, 'seq', split_axis=0, concat_axis=0, tiled=True)  6.35 us
    all_to_all x1, starting transfers between devices, on_device(): lax.all_to_all(pack(selector, neighbour_states, shards, capacity), 'seq',...  3.45 us
  transfers between devices with their start and end apart: 5, of which 4 were waited for; matrix products, arithmetic and copies ran while one was open for 13% of the time, Pallas kernels for 0%

commit v1 on v0

--- a/solution.py
+++ b/solution.py
@@ -7,6 +7,18 @@
 SEGLEN = 64
 NLEN = 64
 NEIGH = 2
+
+
+def collect(x, axis, dim):
+    ways, here = (lax.axis_size(axis), lax.axis_index(axis))
+    grown, reach = (x, 1)
+    while reach < ways:
+        theirs = lax.ppermute(grown, axis, [(d, d ^ reach) for d in range(ways)])
+        mine_first = jnp.concatenate([grown, theirs], axis=dim)
+        theirs_first = jnp.concatenate([theirs, grown], axis=dim)
+        grown = jnp.where(here & reach == 0, mine_first, theirs_first)
+        reach = 2 * reach
+    return grown
 
 
 def shifted(shard, axis, by):
@@ -110,7 +122,7 @@
         lax.all_to_all(sent_dest, "seq", split_axis=0, concat_axis=0, tiled=True),
     )
     arranged = unpack(received, received_dest, own_index, per_shard)
-    routed = lax.all_gather(arranged, ("phase", "mp"), axis=1, tiled=True)
+    routed = collect(arranged, ("phase", "mp"), 1)
     neighbours = normalize(routed, enc_gain)
     key_mat = key_weight[0]
     value_mat = value_weight[0]

time: 138 us -> 126 us (0.913)
  between operations: 13.7 us -> 0.34 us
  waiting for transfers between devices: 41.9 us -> 45.6 us
  other arithmetic: 11.6 us -> 9.35 us
    ppermute x0 -> x3, waiting for transfers between devices: none -> 30.4 us  [collect(): theirs = lax.ppermute(grown, axis, [(d, d ^ reach) for d in range(ways)])]
    all_gather x1 -> x0, waiting for transfers between devices: 27 us -> none  [on_device(): routed = lax.all_gather(arranged, ('phase', 'mp'), axis=1, tiled=True)]
    ppermute x0 -> x3, starting transfers between devices: none -> 3.22 us  [collect(): theirs = lax.ppermute(grown, axis, [(d, d ^ reach) for d in range(ways)])]
    ppermute x2, starting transfers between devices: 7.23 us -> 4.51 us  [shifted(): return lax.ppermute(shard, axis, pairs)]
    reduce_sum x1, other arithmetic: 2.22 us -> 0.72 us  [normalize(): meansq = jnp.mean(states * states, axis=-1, keepdims=True)]
  transfers between devices with their start and end apart: 5 -> 7, of which waited for: 4 -> 6; matrix products, arithmetic and copies ran while one was open for 13% -> 14% of each run, Pallas kernels for 0% -> 0%
where the time goes in v1:
time: 126 us; the launch traced here: 125 us
  waiting for transfers between devices  45.6 us (36%)
  matrix products  32.7 us (26%)
  local copies, waits for them, and re-layouts  19.7 us (16%)
  starting transfers between devices  17.7 us (14%)
  other arithmetic  9.35 us (7%)
    ppermute x3, waiting for transfers between devices, collect(): theirs = lax.ppermute(grown, axis, [(d, d ^ reach) for d in range(ways)])  30.4 us
    dot_general x1, matrix products, attend(): jnp.einsum('whqk,wkhd->wqhd', weights, value_four, preferred_element_type...  19.5 us
    unnamed x31, local copies, waits for them, and re-layouts  10.8 us
    dot_general x2, matrix products, project(): jnp.dot(flattened, weight, preferred_element_type=jnp.float32)  9.46 us
    all_to_all x1, waiting for transfers between devices, on_device(): lax.all_to_all(pack(selector, neighbour_states, shards, capacity), 'seq',...  9.13 us
    all_to_all x1, starting transfers between devices, on_device(): lax.all_to_all(sent_dest, 'seq', split_axis=0, concat_axis=0, tiled=True)  6.35 us
    ppermute x2, starting transfers between devices, shifted(): return lax.ppermute(shard, axis, pairs)  4.51 us
    all_to_all x1, starting transfers between devices, on_device(): lax.all_to_all(pack(selector, neighbour_states, shards, capacity), 'seq',...  3.59 us
  transfers between devices with their start and end apart: 7, of which 6 were waited for; matrix products, arithmetic and copies ran while one was open for 14% of the time, Pallas kernels for 0%

profile of v1, /device:TPU:0, one launch (start us, length us, event | category | flops | bytes accessed | tf_op | source)
XLA Modules:
  0.0 125.3 jit_solution(7274025570280008256)
XLA Ops:
  0.0 0.7 broadcast_add_fusion.1
  0.7 0.2 convert_reduce_fusion
  0.8 0.7 compare_select_fusion.4
  1.5 0.1 select_reduce_fusion
  1.6 0.7 sub.37
  2.3 6.3 %all-to-all-start = ((s32[4,1,5]{2,1,0:T(1,128)}), s32[4,1,5]{2,1,0:T(1,128)S(1)}, u32[]{:S(2)}, u32[]{:S(2)}) async-start(s32[4,1,5]{2,1,0:T(1,128)} %bitcast), calls=%async_computation | async-start | bytes 4096 | tf_op jit(solution)/shard_map/all_to_all | solution.py:122
  8.7 1.0 pad.19
  9.7 0.2 copy.32
  9.9 0.3 convolution_convert_fusion
  10.2 0.2 copy.33
  10.4 0.7 slice.17
  11.1 2.9 %all-to-all-done = s32[4,1,5]{2,1,0:T(1,128)S(1)} async-done(((s32[4,1,5]{2,1,0:T(1,128)}), s32[4,1,5]{2,1,0:T(1,128)S(1)}, u32[]{:S(2)}, u32[]{:S(2)}) %all-to-all-start) | async-done | bytes 112 | tf_op jit(solution)/shard_map/all_to_all | solution.py:122
  14.1 3.6 %all-to-all-start.1 = ((bf16[4,5,8,1024]{3,2,1,0:T(8,128)(2,1)}), bf16[4,5,8,1024]{3,2,1,0:T(8,128)(2,1)S(1)}, u32[]{:S(2)}, u32[]{:S(2)}) async-start(bf16[4,5,8,1024]{3,2,1,0:T(8,128)(2,1)} %bitcast.17), calls=%async_computation.1 | async-start | bytes 655360 | tf_op jit(solution)/shard_map/all_to_all | solution.py:115
  17.7 0.1 select_n.96
  17.8 9.1 %all-to-all-done.1 = bf16[4,5,8,1024]{3,2,1,0:T(8,128)(2,1)S(1)} async-done(((bf16[4,5,8,1024]{3,2,1,0:T(8,128)(2,1)}), bf16[4,5,8,1024]{3,2,1,0:T(8,128)(2,1)S(1)}, u32[]{:S(2)}, u32[]{:S(2)}) %all-to-all-start.1) | async-done | bytes 327712 | tf_op jit(solution)/shard_map/all_to_all | solution.py:115
  27.0 0.2 copy.34
  27.2 0.2 convolution_convert_fusion.1
  27.4 0.2 copy.35
  27.6 1.6 %collective-permute-start = (bf16[16,8,1024]{2,1,0:T(8,128)(2,1)S(1)}, bf16[16,8,1024]{2,1,0:T(8,128)(2,1)S(1)}, u32[]{:S(2)}, u32[]{:S(2)}) collective-permute-start(bf16[16,8,1024]{2,1,0:T(8,128)(2,1)S(1)} %bitcast.76), channel_id=1, source_target_pairs={{0,1},{1,0},{8,9},{9,8},{16,17},{17,16},{24,25},{25,24},{2,3},{3,2... | collective-permute-start | bytes 786440 | tf_op jit(solution)/shard_map/ppermute | solution.py:16
  29.2 4.8 %collective-permute-done = bf16[16,8,1024]{2,1,0:T(8,128)(2,1)S(1)} collective-permute-done((bf16[16,8,1024]{2,1,0:T(8,128)(2,1)S(1)}, bf16[16,8,1024]{2,1,0:T(8,128)(2,1)S(1)}, u32[]{:S(2)}, u32[]{:S(2)}) %collective-permute-start) | collective-permute-done | bytes 262176 | tf_op jit(solution)/shard_map/ppermute | solution.py:16
  34.0 0.1 maximum_select_fusion.2
  34.1 0.1 collective-permute-start.1
  34.2 1.9 %collective-permute-done.1 = bf16[16,16,1024]{2,1,0:T(8,128)(2,1)S(1)} collective-permute-done((bf16[16,16,1024]{2,1,0:T(8,128)(2,1)S(1)}, bf16[16,16,1024]{2,1,0:T(8,128)(2,1)S(1)}, u32[]{:S(2)}, u32[]{:S(2)}) %collective-permute-start.1) | collective-permute-done | bytes 524320 | tf_op jit(solution)/shard_map/ppermute | solution.py:16
  36.1 0.5 maximum_select_fusion.1
  36.6 1.6 %collective-permute-start.2 = (bf16[16,32,1024]{2,1,0:T(8,128)(2,1)S(1)}, bf16[16,32,1024]{2,1,0:T(8,128)(2,1)S(1)}, u32[]{:S(2)}, u32[]{:S(2)}) collective-permute-start(bf16[16,32,1024]{2,1,0:T(8,128)(2,1)S(1)} %maximum_select_fusion.1), channel_id=1, source_target_pairs={{0,16},{1,17},{8,24},{9,25},{16,0},{17,1},{24,8},{25,9},{2,18},{3,... | collective-permute-start | bytes 3145736 | tf_op jit(solution)/shard_map/ppermute | solution.py:16
  38.2 23.7 %collective-permute-done.2 = bf16[16,32,1024]{2,1,0:T(8,128)(2,1)S(1)} collective-permute-done((bf16[16,32,1024]{2,1,0:T(8,128)(2,1)S(1)}, bf16[16,32,1024]{2,1,0:T(8,128)(2,1)S(1)}, u32[]{:S(2)}, u32[]{:S(2)}) %collective-permute-start.2) | collective-permute-done | bytes 1048608 | tf_op jit(solution)/shard_map/ppermute | solution.py:16
  61.9 0.7 fusion.9
  62.6 0.0 copy-done.6
  62.6 0.8 fusion.11
  63.4 0.0 copy-done.7
  63.4 0.0 copy-start.8
  63.4 4.7 %fusion.20 = bf16[1024,2048]{1,0:T(8,128)(2,1)S(1)} fusion(bf16[1024,1024]{1,0:T(8,128)(2,1)S(1)} %bitcast.64, bf16[1,1024,2048]{2,1,0:T(8,128)(2,1)S(1)} %copy-done.7), kind=kOutput, calls=%fused_computation.25 | convolution fusion | flops 4297064448 | bytes 10485760 | tf_op jit(solution)/shard_map/dot_general | solution.py:38
  68.2 0.0 copy-start
  68.2 0.9 slice.14
  69.1 2.0 %collective-permute-start.4 = (bf16[128,2048]{1,0:T(8,128)(2,1)}, bf16[128,2048]{1,0:T(8,128)(2,1)S(1)}, u32[]{:S(2)}, u32[]{:S(2)}) collective-permute-start(bf16[128,2048]{1,0:T(8,128)(2,1)} %slice.14), channel_id=1, source_target_pairs={{0,2},{2,4},{4,6},{1,3},{3,5},{5,7},{8,10},{10,12},{12,14},{9,11},... | collective-permute-start | bytes 1572872 | tf_op jit(solution)/shard_map/ppermute | solution.py:27
  71.1 0.0 copy-done.8
  71.1 4.7 %fusion.17 = bf16[1024,2048]{1,0:T(8,128)(2,1)S(1)} fusion(bf16[1024,1024]{1,0:T(8,128)(2,1)S(1)} %bitcast.65, bf16[1,1024,2048]{2,1,0:T(8,128)(2,1)S(1)} %copy-done.8), kind=kOutput, calls=%fused_computation.24 | convolution fusion | flops 4297064448 | bytes 10485760 | tf_op jit(solution)/shard_map/dot_general | solution.py:38
  75.9 0.0 copy-done
  75.9 0.0 copy-start.2
  75.9 0.9 slice.15
  76.8 1.3 %copy-done.2 = bf16[1024,2048]{1,0:T(8,128)(2,1)} copy-done((bf16[1024,2048]{1,0:T(8,128)(2,1)}, bf16[1024,2048]{1,0:T(8,128)(2,1)S(1)}, u32[]{:S(2)}) %copy-start.2) | copy-done | bytes 4194328
  78.1 2.5 %collective-permute-start.3 = (bf16[128,2048]{1,0:T(8,128)(2,1)}, bf16[128,2048]{1,0:T(8,128)(2,1)S(1)}, u32[]{:S(2)}, u32[]{:S(2)}) collective-permute-start(bf16[128,2048]{1,0:T(8,128)(2,1)} %slice.15), channel_id=1, source_target_pairs={{0,2},{2,4},{4,6},{1,3},{3,5},{5,7},{8,10},{10,12},{12,14},{9,11},... | collective-permute-start | bytes 1572872 | tf_op jit(solution)/shard_map/ppermute | solution.py:27
  80.5 0.1 pad.18.clone
  80.6 1.0 maximum_bitcast_fusion
  81.7 0.7 copy.31
  82.4 0.4 copy-done.3
  82.8 1.4 %copy.39 = bf16[128,8,16,128]{3,2,1,0:T(8,128)(2,1)S(1)} copy(bf16[128,8,16,128]{3,1,2,0:T(8,128)(2,1)S(1)} %bitcast.62) | data formatting | bytes 8388608
  84.2 0.0 copy-start.1
  84.2 3.2 %copy.26 = bf16[8,128,16,128]{3,1,2,0:T(8,128)(2,1)} copy(bf16[8,128,16,128]{3,2,1,0:T(8,128)(2,1)S(1)} %bitcast.56) | data formatting | bytes 8388608 | tf_op jit(solution)/shard_map/concatenate | solution.py:100
  87.4 1.4 %copy.37 = bf16[128,8,16,128]{3,2,1,0:T(8,128)(2,1)S(1)} copy(bf16[128,8,16,128]{3,1,2,0:T(8,128)(2,1)S(1)} %bitcast.61) | data formatting | bytes 8388608
  88.8 1.2 copy.28
  90.0 0.0 collective-permute-done.4
  90.0 0.1 copy.36
  90.2 0.1 copy.27
  90.3 3.1 %collective-permute-done.3 = bf16[128,2048]{1,0:T(8,128)(2,1)S(1)} collective-permute-done((bf16[128,2048]{1,0:T(8,128)(2,1)}, bf16[128,2048]{1,0:T(8,128)(2,1)S(1)}, u32[]{:S(2)}, u32[]{:S(2)}) %collective-permute-start.3) | collective-permute-done | bytes 524320 | tf_op jit(solution)/shard_map/ppermute | solution.py:27
  93.4 0.1 copy.38
  93.5 0.1 copy.25
  93.6 3.3 %fusion.1 = f32[9,16,64,128]{3,2,1,0:T(8,128)S(1)} fusion(bf16[8,128,16,128]{3,1,2,0:T(8,128)(2,1)S(1)} %copy.28, bf16[1,128,16,128]{3,1,2,0:T(8,128)(2,1)S(1)} %copy.27, bf16[9,64,16,128]{3,2,1,0:T(8,128)(2,1)S(1)} %bitcast.59), kind=kOutput, calls=%fused_computation.5 | convolution fusion | flops 304349184 | bytes 11796480 | tf_op jit(solution)/shard_map/wqhd,wkhd->whqk/dot_general | solution.py:47
  97.0 2.1 %copy-done.4 = f32[9,16,64,128]{3,2,1,0:T(8,128)} copy-done((f32[9,16,64,128]{3,2,1,0:T(8,128)}, f32[9,16,64,128]{3,2,1,0:T(8,128)S(1)}, u32[]{:S(2)}) %copy-start.4) | copy-done | bytes 4718616
  99.1 2.5 %fusion.51 = f32[9,16,64]{2,1,0:T(8,128)S(1)} fusion(f32[9,16,64,128]{3,2,1,0:T(8,128)S(1)} %fusion.1), kind=kOutput, calls=%fused_computation.74 | output fusion | flops 4718719 | bytes 4755456 | tf_op jit(solution)/shard_map/sub | solution.py:51
  101.6 19.5 %convert_bitcast_fusion = bf16[9,64,16,128]{3,1,2,0:T(8,128)(2,1)S(1)} fusion(bf16[8,128,16,128]{3,1,2,0:T(8,128)(2,1)} %copy.26, bf16[1,128,16,128]{3,1,2,0:T(8,128)(2,1)S(1)} %copy.25, f32[9,16,64]{2,1,0:T(8,128)S(1)} %fusion.51, f32[9,16,64,128]{3,2,1,0:T(8,128)} %copy-done.4), kind=kOutput, calls=%fused_computation.29 | convolution fusion | flops 318514304 | bytes 11833344 | tf_op jit(solution)/shard_map/whqk,wkhd->wqhd/dot_general | solution.py:53
  121.1 1.6 %copy.30 = bf16[9,64,16,128]{3,2,1,0:T(8,128)(2,1)S(1)} copy(bf16[9,64,16,128]{3,1,2,0:T(8,128)(2,1)S(1)} %convert_bitcast_fusion) | data formatting | bytes 4718592 | tf_op jit(solution)/shard_map/convert_element_type | solution.py:54
  122.7 0.6 copy.44
  123.3 2.0 %fusion.28 = bf16[1,512,2048]{2,1,0:T(8,128)(2,1)} fusion(bf16[576,2048]{1,0:T(8,128)(2,1)S(1)} %bitcast.60, pred[512]{0:T(512)(128)(4,1)S(1)} %fusion.44), kind=kLoop, calls=%fused_computation.33 | loop fusion | flops 1048576 | bytes 4194816 | tf_op jit(solution)/shard_map/broadcast_in_dim | solution.py:138
  (14 shorter events, 0.1 us)
Async XLA Ops:
  2.3 11.8 %all-to-all-start = ((s32[4,1,5]{2,1,0:T(1,128)}), s32[4,1,5]{2,1,0:T(1,128)S(1)}, u32[]{:S(2)}, u32[]{:S(2)}) async-start(s32[4,1,5]{2,1,0:T(1,128)} %bitcast), calls=%async_computation | async-start | bytes 4096 | tf_op jit(solution)/shard_map/all_to_all | solution.py:122
  14.1 48.5 %copy-start.6 = (f32[1024]{0:T(1024)S(1)}, f32[1024]{0:T(1024)}, u32[]{:S(2)}) copy-start(f32[1024]{0:T(1024)} %param.9) | copy-start | bytes 12292
  14.1 12.8 %all-to-all-start.1 = ((bf16[4,5,8,1024]{3,2,1,0:T(8,128)(2,1)}), bf16[4,5,8,1024]{3,2,1,0:T(8,128)(2,1)S(1)}, u32[]{:S(2)}, u32[]{:S(2)}) async-start(bf16[4,5,8,1024]{3,2,1,0:T(8,128)(2,1)} %bitcast.17), calls=%async_computation.1 | async-start | bytes 655360 | tf_op jit(solution)/shard_map/all_to_all | solution.py:115
  27.6 6.4 %collective-permute-start = (bf16[16,8,1024]{2,1,0:T(8,128)(2,1)S(1)}, bf16[16,8,1024]{2,1,0:T(8,128)(2,1)S(1)}, u32[]{:S(2)}, u32[]{:S(2)}) collective-permute-start(bf16[16,8,1024]{2,1,0:T(8,128)(2,1)S(1)} %bitcast.76), channel_id=1, source_target_pairs={{0,1},{1,0},{8,9},{9,8},{16,17},{17,16},{24,25},{25,24},{2,3},{3,2... | collective-permute-start | bytes 786440 | tf_op jit(solution)/shard_map/ppermute | solution.py:16
  34.1 2.0 %collective-permute-start.1 = (bf16[16,16,1024]{2,1,0:T(8,128)(2,1)S(1)}, bf16[16,16,1024]{2,1,0:T(8,128)(2,1)S(1)}, u32[]{:S(2)}, u32[]{:S(2)}) collective-permute-start(bf16[16,16,1024]{2,1,0:T(8,128)(2,1)S(1)} %maximum_select_fusion.2), channel_id=1, source_target_pairs={{0,8},{1,9},{8,0},{9,1},{16,24},{17,25},{24,16},{25,17},{2,10},{3,... | collective-permute-start | bytes 1572872 | tf_op jit(solution)/shard_map/ppermute | solution.py:16
  36.6 25.3 %collective-permute-start.2 = (bf16[16,32,1024]{2,1,0:T(8,128)(2,1)S(1)}, bf16[16,32,1024]{2,1,0:T(8,128)(2,1)S(1)}, u32[]{:S(2)}, u32[]{:S(2)}) collective-permute-start(bf16[16,32,1024]{2,1,0:T(8,128)(2,1)S(1)} %maximum_select_fusion.1), channel_id=1, source_target_pairs={{0,16},{1,17},{8,24},{9,25},{16,0},{17,1},{24,8},{25,9},{2,18},{3,... | collective-permute-start | bytes 3145736 | tf_op jit(solution)/shard_map/ppermute | solution.py:16
  38.2 25.3 %copy-start.7 = (bf16[1,1024,2048]{2,1,0:T(8,128)(2,1)S(1)}, bf16[1,1024,2048]{2,1,0:T(8,128)(2,1)}, u32[]{:S(2)}) copy-start(bf16[1,1024,2048]{2,1,0:T(8,128)(2,1)} %param.7) | copy-start | bytes 12582916
  63.4 7.7 %copy-start.8 = (bf16[1,1024,2048]{2,1,0:T(8,128)(2,1)S(1)}, bf16[1,1024,2048]{2,1,0:T(8,128)(2,1)}, u32[]{:S(2)}) copy-start(bf16[1,1024,2048]{2,1,0:T(8,128)(2,1)} %param.8) | copy-start | bytes 12582916
  68.2 7.7 %copy-start = (bf16[1024,2048]{1,0:T(8,128)(2,1)}, bf16[1024,2048]{1,0:T(8,128)(2,1)S(1)}, u32[]{:S(2)}) copy-start(bf16[1024,2048]{1,0:T(8,128)(2,1)S(1)} %fusion.20) | copy-start | bytes 12582916
  69.1 11.6 %copy-start.5 = (bf16[1,512,2048]{2,1,0:T(8,128)(2,1)S(1)}, bf16[1,512,2048]{2,1,0:T(8,128)(2,1)}, u32[]{:S(2)}) copy-start(bf16[1,512,2048]{2,1,0:T(8,128)(2,1)} %param.6) | copy-start | bytes 6291460
  69.1 21.0 %collective-permute-start.4 = (bf16[128,2048]{1,0:T(8,128)(2,1)}, bf16[128,2048]{1,0:T(8,128)(2,1)S(1)}, u32[]{:S(2)}, u32[]{:S(2)}) collective-permute-start(bf16[128,2048]{1,0:T(8,128)(2,1)} %slice.14), channel_id=1, source_target_pairs={{0,2},{2,4},{4,6},{1,3},{3,5},{5,7},{8,10},{10,12},{12,14},{9,11},... | collective-permute-start | bytes 1572872 | tf_op jit(solution)/shard_map/ppermute | solution.py:27
  75.9 2.2 %copy-start.2 = (bf16[1024,2048]{1,0:T(8,128)(2,1)}, bf16[1024,2048]{1,0:T(8,128)(2,1)S(1)}, u32[]{:S(2)}) copy-start(bf16[1024,2048]{1,0:T(8,128)(2,1)S(1)} %fusion.17) | copy-start | bytes 12582916
  78.1 15.3 %collective-permute-start.3 = (bf16[128,2048]{1,0:T(8,128)(2,1)}, bf16[128,2048]{1,0:T(8,128)(2,1)S(1)}, u32[]{:S(2)}, u32[]{:S(2)}) collective-permute-start(bf16[128,2048]{1,0:T(8,128)(2,1)} %slice.15), channel_id=1, source_target_pairs={{0,2},{2,4},{4,6},{1,3},{3,5},{5,7},{8,10},{10,12},{12,14},{9,11},... | collective-permute-start | bytes 1572872 | tf_op jit(solution)/shard_map/ppermute | solution.py:27
  80.6 2.2 %copy-start.3 = (bf16[1024,2048]{1,0:T(8,128)(2,1)S(1)}, bf16[1024,2048]{1,0:T(8,128)(2,1)}, u32[]{:S(2)}) copy-start(bf16[1024,2048]{1,0:T(8,128)(2,1)} %copy-done.2) | copy-start | bytes 12582916
  84.2 3.2 %copy-start.1 = (bf16[1024,2048]{1,0:T(8,128)(2,1)S(1)}, bf16[1024,2048]{1,0:T(8,128)(2,1)}, u32[]{:S(2)}) copy-start(bf16[1024,2048]{1,0:T(8,128)(2,1)} %copy-done) | copy-start | bytes 12582916
  96.9 2.1 %copy-start.4 = (f32[9,16,64,128]{3,2,1,0:T(8,128)}, f32[9,16,64,128]{3,2,1,0:T(8,128)S(1)}, u32[]{:S(2)}) copy-start(f32[9,16,64,128]{3,2,1,0:T(8,128)S(1)} %fusion.1) | copy-start | bytes 14155780
